TPU v7x, 128 devices: a whole 4x4x4 slice. The times are simulated.
128 devices in a mesh: az: 16 (over z, x_hi, core), dep: 8 (over y, x_lo).
Axes of the slice: x: 4 (x_hi: 2, x_lo: 2; x = x_hi * 2 + x_lo), y: 4, z: 4, core: 2. Of those that a mesh axis runs over, the one named last changes fastest.
Arguments:
- adjoint_in: float32 [2, 2048, 4096], P(None, 'az', 'dep'), may hold values from -6 to 6
- forward_field: float32 [8, 2, 2048, 4096], P(None, None, 'az', 'dep'), may hold values from -6 to 6
- screen: float32 [2048, 4096], P('az', 'dep'), may hold values from -3.140625 to 3.140625
- bed_weight: float32 [4096], replicated, may hold values from 0.1 to 1
- labels: int32 [2048, 32], P('az'), may hold values from 0 to 31
Outputs:
- adjoint_out: float32 [2, 2048, 4096], P(None, 'az', 'dep')
- sensitivity: float32 [32], replicated
All inputs are finite; a program needn't handle non-finite values.
Results may differ from a plain program's by a relative error of at most 0.0003.
Values sent between devices are 32-bit elements; how exact they have to be, the bound alone decides.
No kernel may reach another device: no remote copies, remote signals or barrier semaphores. Data moves between devices by JAX's collectives and lax.ppermute only.
A program may use at most 128 MiB of HBM per device.

v0:
```python
import math
import jax
import jax.numpy as jnp
from jax import lax
from jax.sharding import PartitionSpec as P

GROUPS = 32
coupling = 0.15
radix_rows = 64
label_block = 128
highest = lax.Precision.HIGHEST


def padded_2(cells, sides, width):
    for axis, dim in sides:
        count = lax.axis_size(axis)
        head = lax.slice_in_dim(cells, 0, width, axis=dim)
        tail = lax.slice_in_dim(cells, cells.shape[dim] - width, cells.shape[dim], axis=dim)
        cells = jnp.concatenate(
            [
                lax.ppermute(tail, axis, [(i, (i + 1) % count) for i in range(count)]),
                cells,
                lax.ppermute(head, axis, [((i + 1) % count, i) for i in range(count)]),
            ],
            axis=dim,
        )
    return cells


def angles(left, right, modulus, sign):
    product = left[:, None] * right[None, :] % modulus
    return sign * 2.0 * math.pi * product.astype(jnp.float32) / modulus


def combine(form, real_part, imag_part, cosine, sine):
    first = jnp.einsum(form, real_part, cosine, precision=highest) - jnp.einsum(
        form, imag_part, sine, precision=highest
    )
    second = jnp.einsum(form, real_part, sine, precision=highest) + jnp.einsum(
        form, imag_part, cosine, precision=highest
    )
    return (first, second)


def transform(real_part, imag_part, sign):
    length = real_part.shape[-1]
    second_len = length // radix_rows
    leading = real_part.shape[:-1]
    shaped_re = real_part.reshape(leading + (radix_rows, second_len))
    shaped_im = imag_part.reshape(leading + (radix_rows, second_len))
    outer_idx = jnp.arange(radix_rows, dtype=jnp.int32)
    inner_idx = jnp.arange(second_len, dtype=jnp.int32)
    first_ang = angles(outer_idx, outer_idx, radix_rows, sign)
    mid_re, mid_im = combine(
        "...ab,ac->...cb", shaped_re, shaped_im, jnp.cos(first_ang), jnp.sin(first_ang)
    )
    twist = angles(outer_idx, inner_idx, length, sign)
    twist_c = jnp.cos(twist)
    twist_s = jnp.sin(twist)
    mid_re, mid_im = (mid_re * twist_c - mid_im * twist_s, mid_re * twist_s + mid_im * twist_c)
    last_ang = angles(inner_idx, inner_idx, second_len, sign)
    out_re, out_im = combine(
        "...cb,bd->...dc", mid_re, mid_im, jnp.cos(last_ang), jnp.sin(last_ang)
    )
    return (out_re.reshape(leading + (length,)), out_im.reshape(leading + (length,)))


def propagate(field):
    length = field.shape[-1]
    freq = jnp.arange(length, dtype=jnp.int32)
    freq = jnp.where(freq < length // 2, freq, freq - length).astype(jnp.float32)
    beta = 30.0 * (freq / (length // 2)) ** 2
    spec_re, spec_im = transform(field[0], field[1], -1.0)
    cos_b = jnp.cos(beta)
    sin_b = jnp.sin(beta)
    turned_re = spec_re * cos_b - spec_im * sin_b
    turned_im = spec_re * sin_b + spec_im * cos_b
    back_re, back_im = transform(turned_re, turned_im, 1.0)
    return jnp.stack([back_re, back_im]) / length


def couple(padded):
    lap_wide = padded[:, :-2] + padded[:, 2:] - 2.0 * padded[:, 1:-1]
    lap = lap_wide[:, 1:-1]
    lap_two = lap_wide[:, :-2] + lap_wide[:, 2:] - 2.0 * lap
    centre = padded[:, 2:-2]
    half = 0.5 * coupling * coupling
    new_re = centre[0] + coupling * lap[1] - half * lap_two[0]
    new_im = centre[1] - coupling * lap[0] - half * lap_two[1]
    return jnp.stack([new_re, new_im])


def group_table(marks):
    return (marks[:, :, None] == jnp.arange(GROUPS, dtype=jnp.int32)[None, None, :]).astype(
        jnp.float32
    )


def group_terms(field, stored_step, weight, onehot):
    term = (field[1] * stored_step[0] - field[0] * stored_step[1]) * weight[None, :]
    blocks = term.reshape(term.shape[0], -1, label_block).sum(-1)
    return jnp.einsum("rb,rbg->g", blocks, onehot, precision=highest)


def rotate(field, cosine, sine):
    return jnp.stack([field[0] * cosine + field[1] * sine, field[1] * cosine - field[0] * sine])


def on_device(adjoint_in, forward_field, screen, bed_weight, labels):
    steps = forward_field.shape[0]
    dep_rank = lax.axis_index("dep")
    cols_here = adjoint_in.shape[2]
    count_blocks = cols_here // label_block
    sensitivity = jnp.zeros((GROUPS,), jnp.float32)
    field = adjoint_in
    weight_cols = lax.dynamic_slice_in_dim(bed_weight, dep_rank * cols_here, cols_here, 0)
    onehot_cols = group_table(
        lax.dynamic_slice_in_dim(labels, dep_rank * count_blocks, count_blocks, 1)
    )
    cosine = jnp.cos(screen)
    sine = jnp.sin(screen)
    for step in range(steps - 1, -1, -1):
        sensitivity = sensitivity + group_terms(
            field, forward_field[step], weight_cols, onehot_cols
        )
        padded = padded_2(rotate(field, cosine, sine), (("az", 1),), 2)
        deep = lax.all_to_all(couple(padded), "dep", split_axis=1, concat_axis=2, tiled=True)
        field = lax.all_to_all(propagate(deep), "dep", split_axis=2, concat_axis=1, tiled=True)
    total = lax.psum(sensitivity, ("az", "dep"))
    return (field, total)


def solution(mesh):
    return jax.shard_map(
        on_device,
        mesh=mesh,
        in_specs=(
            P(None, "az", "dep"),
            P(None, None, "az", "dep"),
            P("az", "dep"),
            P(),
            P("az", None),
        ),
        out_specs=(P(None, "az", "dep"), P()),
        check_vma=False,
    )
```

profile of v0, /device:TPU:1, one launch (start us, length us, event | category | flops | bytes accessed | tf_op | source)
XLA Modules:
  0.0 805.0 jit_solution(5096109944816775397)
XLA Ops:
  58.6 10.0 %all_to_all.243 = f32[8,1,16384]{2,1,0:T(1,128)S(1)} all-to-all(f32[8,1,16384]{2,1,0:T(1,128)S(1)} %reshape.596), channel_id=1, replica_groups=mesh['az'=16,'dep'=8] {'dep'}, dimensions={0} | all-to-all | bytes 1048576 | tf_op jit(solution)/shard_map/all_to_all | solution.py:128
  70.8 7.5 reshape.597
  83.7 8.8 %collective-permute-start.3 = (f32[2,2,512]{2,1,0:T(2,128)S(1)}, f32[2,2,512]{2,1,0:T(2,128)S(1)}, u32[]{:S(2)}, u32[]{:S(2)}) collective-permute-start(f32[2,2,512]{2,1,0:T(2,128)S(1)} %get-tuple-element.107), channel_id=1, source_target_pairs={{8,0},{16,8},{24,16},{32,24},{40,32},{48,40},{56,48},{64,56},{72,6... | collective-permute-start | bytes 24584 | tf_op jit(solution)/shard_map/ppermute | solution.py:23
  96.7 10.0 %all_to_all.244 = f32[2,128,512]{2,0,1:T(2,128)S(1)} all-to-all(f32[2,128,512]{2,0,1:T(2,128)S(1)} %copy.134), channel_id=1, replica_groups=mesh['az'=16,'dep'=8] {'dep'}, dimensions={1} | all-to-all | bytes 1048576 | tf_op jit(solution)/shard_map/all_to_all | solution.py:127
  141.1 10.0 %all_to_all.245 = f32[8,1,16384]{2,1,0:T(1,128)S(1)} all-to-all(f32[8,1,16384]{2,1,0:T(1,128)S(1)} %reshape.598), channel_id=1, replica_groups=mesh['az'=16,'dep'=8] {'dep'}, dimensions={0} | all-to-all | bytes 1048576 | tf_op jit(solution)/shard_map/all_to_all | solution.py:128
  165.7 8.7 %collective-permute-start.5 = (f32[2,2,512]{2,1,0:T(2,128)S(1)}, f32[2,2,512]{2,1,0:T(2,128)S(1)}, u32[]{:S(2)}, u32[]{:S(2)}) collective-permute-start(f32[2,2,512]{2,1,0:T(2,128)S(1)} %get-tuple-element.101), channel_id=1, source_target_pairs={{8,0},{16,8},{24,16},{32,24},{40,32},{48,40},{56,48},{64,56},{72,6... | collective-permute-start | bytes 24584 | tf_op jit(solution)/shard_map/ppermute | solution.py:23
  178.4 10.0 %all_to_all.246 = f32[2,128,512]{2,0,1:T(2,128)S(1)} all-to-all(f32[2,128,512]{2,0,1:T(2,128)S(1)} %copy.138), channel_id=1, replica_groups=mesh['az'=16,'dep'=8] {'dep'}, dimensions={1} | all-to-all | bytes 1048576 | tf_op jit(solution)/shard_map/all_to_all | solution.py:127
  228.1 10.0 %all_to_all.247 = f32[8,1,16384]{2,1,0:T(1,128)S(1)} all-to-all(f32[8,1,16384]{2,1,0:T(1,128)S(1)} %reshape.600), channel_id=1, replica_groups=mesh['az'=16,'dep'=8] {'dep'}, dimensions={0} | all-to-all | bytes 1048576 | tf_op jit(solution)/shard_map/all_to_all | solution.py:128
  252.7 8.7 %collective-permute-start.7 = (f32[2,2,512]{2,1,0:T(2,128)S(1)}, f32[2,2,512]{2,1,0:T(2,128)S(1)}, u32[]{:S(2)}, u32[]{:S(2)}) collective-permute-start(f32[2,2,512]{2,1,0:T(2,128)S(1)} %get-tuple-element.95), channel_id=1, source_target_pairs={{8,0},{16,8},{24,16},{32,24},{40,32},{48,40},{56,48},{64,56},{72,6... | collective-permute-start | bytes 24584 | tf_op jit(solution)/shard_map/ppermute | solution.py:23
  265.4 10.0 %all_to_all.248 = f32[2,128,512]{2,0,1:T(2,128)S(1)} all-to-all(f32[2,128,512]{2,0,1:T(2,128)S(1)} %copy.142), channel_id=1, replica_groups=mesh['az'=16,'dep'=8] {'dep'}, dimensions={1} | all-to-all | bytes 1048576 | tf_op jit(solution)/shard_map/all_to_all | solution.py:127
  318.8 10.0 %all_to_all.249 = f32[8,1,16384]{2,1,0:T(1,128)S(1)} all-to-all(f32[8,1,16384]{2,1,0:T(1,128)S(1)} %reshape.602), channel_id=1, replica_groups=mesh['az'=16,'dep'=8] {'dep'}, dimensions={0} | all-to-all | bytes 1048576 | tf_op jit(solution)/shard_map/all_to_all | solution.py:128
  343.4 8.7 %collective-permute-start.9 = (f32[2,2,512]{2,1,0:T(2,128)S(1)}, f32[2,2,512]{2,1,0:T(2,128)S(1)}, u32[]{:S(2)}, u32[]{:S(2)}) collective-permute-start(f32[2,2,512]{2,1,0:T(2,128)S(1)} %get-tuple-element.89), channel_id=1, source_target_pairs={{8,0},{16,8},{24,16},{32,24},{40,32},{48,40},{56,48},{64,56},{72,6... | collective-permute-start | bytes 24584 | tf_op jit(solution)/shard_map/ppermute | solution.py:23
  356.4 10.0 %all_to_all.250 = f32[2,128,512]{2,0,1:T(2,128)S(1)} all-to-all(f32[2,128,512]{2,0,1:T(2,128)S(1)} %copy.146), channel_id=1, replica_groups=mesh['az'=16,'dep'=8] {'dep'}, dimensions={1} | all-to-all | bytes 1048576 | tf_op jit(solution)/shard_map/all_to_all | solution.py:127
  409.8 10.0 %all_to_all.251 = f32[8,1,16384]{2,1,0:T(1,128)S(1)} all-to-all(f32[8,1,16384]{2,1,0:T(1,128)S(1)} %reshape.604), channel_id=1, replica_groups=mesh['az'=16,'dep'=8] {'dep'}, dimensions={0} | all-to-all | bytes 1048576 | tf_op jit(solution)/shard_map/all_to_all | solution.py:128
  434.4 8.6 %collective-permute-start.11 = (f32[2,2,512]{2,1,0:T(2,128)S(1)}, f32[2,2,512]{2,1,0:T(2,128)S(1)}, u32[]{:S(2)}, u32[]{:S(2)}) collective-permute-start(f32[2,2,512]{2,1,0:T(2,128)S(1)} %get-tuple-element.83), channel_id=1, source_target_pairs={{8,0},{16,8},{24,16},{32,24},{40,32},{48,40},{56,48},{64,56},{72,6... | collective-permute-start | bytes 24584 | tf_op jit(solution)/shard_map/ppermute | solution.py:23
  447.4 10.0 %all_to_all.252 = f32[2,128,512]{2,0,1:T(2,128)S(1)} all-to-all(f32[2,128,512]{2,0,1:T(2,128)S(1)} %copy.150), channel_id=1, replica_groups=mesh['az'=16,'dep'=8] {'dep'}, dimensions={1} | all-to-all | bytes 1048576 | tf_op jit(solution)/shard_map/all_to_all | solution.py:127
  500.8 10.0 %all_to_all.253 = f32[8,1,16384]{2,1,0:T(1,128)S(1)} all-to-all(f32[8,1,16384]{2,1,0:T(1,128)S(1)} %reshape.606), channel_id=1, replica_groups=mesh['az'=16,'dep'=8] {'dep'}, dimensions={0} | all-to-all | bytes 1048576 | tf_op jit(solution)/shard_map/all_to_all | solution.py:128
  525.5 8.7 %collective-permute-start.13 = (f32[2,2,512]{2,1,0:T(2,128)S(1)}, f32[2,2,512]{2,1,0:T(2,128)S(1)}, u32[]{:S(2)}, u32[]{:S(2)}) collective-permute-start(f32[2,2,512]{2,1,0:T(2,128)S(1)} %get-tuple-element.77), channel_id=1, source_target_pairs={{8,0},{16,8},{24,16},{32,24},{40,32},{48,40},{56,48},{64,56},{72,6... | collective-permute-start | bytes 24584 | tf_op jit(solution)/shard_map/ppermute | solution.py:23
  538.5 10.0 %all_to_all.254 = f32[2,128,512]{2,0,1:T(2,128)S(1)} all-to-all(f32[2,128,512]{2,0,1:T(2,128)S(1)} %copy.154), channel_id=1, replica_groups=mesh['az'=16,'dep'=8] {'dep'}, dimensions={1} | all-to-all | bytes 1048576 | tf_op jit(solution)/shard_map/all_to_all | solution.py:127
  584.7 7.9 reshape.608
  618.2 8.5 %collective-permute-start.15 = (f32[2,2,512]{2,1,0:T(2,128)S(1)}, f32[2,2,512]{2,1,0:T(2,128)S(1)}, u32[]{:S(2)}, u32[]{:S(2)}) collective-permute-start(f32[2,2,512]{2,1,0:T(2,128)S(1)} %get-tuple-element.71), channel_id=1, source_target_pairs={{8,0},{16,8},{24,16},{32,24},{40,32},{48,40},{56,48},{64,56},{72,6... | collective-permute-start | bytes 24584 | tf_op jit(solution)/shard_map/ppermute | solution.py:23
  704.5 7.9 reshape.610
  719.1 70.0 %psum.7 = f32[32]{0:T(128)} all-reduce(f32[32]{0:T(128)S(1)} %add_add_fusion), channel_id=1, replica_groups=mesh['az'=16,'dep'=8] {'az','dep'}, use_global_device_ids=true, to_apply=%region_8.9 | all-reduce | flops 32 | bytes 256 | tf_op jit(solution)/shard_map/psum | solution.py:129
  790.9 7.6 reshape.611
  (420 shorter events, 521.7 us)
Async XLA Ops:
  0.6 596.3 %copy-start = (f32[4096]{0:T(1024)S(1)}, f32[4096]{0:T(1024)}, u32[]{:S(2)}) copy-start(f32[4096]{0:T(1024)} %param.8) | copy-start | bytes 49156
  3.7 5.5 collective-permute-start.1
  5.2 6.7 collective-permute-start
  14.0 11.8 %all-to-all-start = ((f32[2,128,512]{2,0,1:T(2,128)}), f32[2,128,512]{2,0,1:T(2,128)S(1)}, u32[]{:S(2)}, u32[]{:S(2)}) async-start(f32[2,128,512]{2,0,1:T(2,128)} %pad_maximum_fusion.24), calls=%async_computation | async-start | bytes 1048576 | tf_op jit(solution)/shard_map/all_to_all | solution.py:127
  83.7 9.6 %collective-permute-start.3 = (f32[2,2,512]{2,1,0:T(2,128)S(1)}, f32[2,2,512]{2,1,0:T(2,128)S(1)}, u32[]{:S(2)}, u32[]{:S(2)}) collective-permute-start(f32[2,2,512]{2,1,0:T(2,128)S(1)} %get-tuple-element.107), channel_id=1, source_target_pairs={{8,0},{16,8},{24,16},{32,24},{40,32},{48,40},{56,48},{64,56},{72,6... | collective-permute-start | bytes 24584 | tf_op jit(solution)/shard_map/ppermute | solution.py:23
  92.5 3.3 collective-permute-start.2
  165.7 9.5 %collective-permute-start.5 = (f32[2,2,512]{2,1,0:T(2,128)S(1)}, f32[2,2,512]{2,1,0:T(2,128)S(1)}, u32[]{:S(2)}, u32[]{:S(2)}) collective-permute-start(f32[2,2,512]{2,1,0:T(2,128)S(1)} %get-tuple-element.101), channel_id=1, source_target_pairs={{8,0},{16,8},{24,16},{32,24},{40,32},{48,40},{56,48},{64,56},{72,6... | collective-permute-start | bytes 24584 | tf_op jit(solution)/shard_map/ppermute | solution.py:23
  174.3 3.2 collective-permute-start.4
  252.7 9.5 %collective-permute-start.7 = (f32[2,2,512]{2,1,0:T(2,128)S(1)}, f32[2,2,512]{2,1,0:T(2,128)S(1)}, u32[]{:S(2)}, u32[]{:S(2)}) collective-permute-start(f32[2,2,512]{2,1,0:T(2,128)S(1)} %get-tuple-element.95), channel_id=1, source_target_pairs={{8,0},{16,8},{24,16},{32,24},{40,32},{48,40},{56,48},{64,56},{72,6... | collective-permute-start | bytes 24584 | tf_op jit(solution)/shard_map/ppermute | solution.py:23
  261.4 3.1 collective-permute-start.6
  343.4 9.5 %collective-permute-start.9 = (f32[2,2,512]{2,1,0:T(2,128)S(1)}, f32[2,2,512]{2,1,0:T(2,128)S(1)}, u32[]{:S(2)}, u32[]{:S(2)}) collective-permute-start(f32[2,2,512]{2,1,0:T(2,128)S(1)} %get-tuple-element.89), channel_id=1, source_target_pairs={{8,0},{16,8},{24,16},{32,24},{40,32},{48,40},{56,48},{64,56},{72,6... | collective-permute-start | bytes 24584 | tf_op jit(solution)/shard_map/ppermute | solution.py:23
  352.1 3.4 collective-permute-start.8
  434.4 9.4 %collective-permute-start.11 = (f32[2,2,512]{2,1,0:T(2,128)S(1)}, f32[2,2,512]{2,1,0:T(2,128)S(1)}, u32[]{:S(2)}, u32[]{:S(2)}) collective-permute-start(f32[2,2,512]{2,1,0:T(2,128)S(1)} %get-tuple-element.83), channel_id=1, source_target_pairs={{8,0},{16,8},{24,16},{32,24},{40,32},{48,40},{56,48},{64,56},{72,6... | collective-permute-start | bytes 24584 | tf_op jit(solution)/shard_map/ppermute | solution.py:23
  443.0 3.5 collective-permute-start.10
  525.5 9.5 %collective-permute-start.13 = (f32[2,2,512]{2,1,0:T(2,128)S(1)}, f32[2,2,512]{2,1,0:T(2,128)S(1)}, u32[]{:S(2)}, u32[]{:S(2)}) collective-permute-start(f32[2,2,512]{2,1,0:T(2,128)S(1)} %get-tuple-element.77), channel_id=1, source_target_pairs={{8,0},{16,8},{24,16},{32,24},{40,32},{48,40},{56,48},{64,56},{72,6... | collective-permute-start | bytes 24584 | tf_op jit(solution)/shard_map/ppermute | solution.py:23
  534.1 3.5 collective-permute-start.12
  592.6 11.0 %all-to-all-start.13 = ((f32[8,1,16384]{2,1,0:T(1,128)}), f32[8,1,16384]{2,1,0:T(1,128)S(1)}, u32[]{:S(2)}, u32[]{:S(2)}) async-start(f32[8,1,16384]{2,1,0:T(1,128)} %reshape.608), calls=%async_computation.13 | async-start | bytes 1048576 | tf_op jit(solution)/shard_map/all_to_all | solution.py:128
  618.2 47.7 %collective-permute-start.15 = (f32[2,2,512]{2,1,0:T(2,128)S(1)}, f32[2,2,512]{2,1,0:T(2,128)S(1)}, u32[]{:S(2)}, u32[]{:S(2)}) collective-permute-start(f32[2,2,512]{2,1,0:T(2,128)S(1)} %get-tuple-element.71), channel_id=1, source_target_pairs={{8,0},{16,8},{24,16},{32,24},{40,32},{48,40},{56,48},{64,56},{72,6... | collective-permute-start | bytes 24584 | tf_op jit(solution)/shard_map/ppermute | solution.py:23
  626.7 39.2 %collective-permute-start.14 = (f32[2,2,512]{2,1,0:T(2,128)S(1)}, f32[2,2,512]{2,1,0:T(2,128)S(1)}, u32[]{:S(2)}, u32[]{:S(2)}) collective-permute-start(f32[2,2,512]{2,1,0:T(2,128)S(1)} %get-tuple-element.70), channel_id=1, source_target_pairs={{0,8},{8,16},{16,24},{24,32},{32,40},{40,48},{48,56},{56,64},{64,7... | collective-permute-start | bytes 24584 | tf_op jit(solution)/shard_map/ppermute | solution.py:21
  642.1 22.3 %copy-start.4 = (f32[1,8,16,512]{3,2,1,0:T(8,128)S(1)}, f32[1,8,16,512]{3,2,1,0:T(8,128)}, u32[]{:S(2)}) copy-start(f32[1,8,16,512]{3,2,1,0:T(8,128)} %copy-done.3) | copy-start | bytes 786436
  643.8 21.3 %copy-start.2 = (f32[1,8,16,512]{3,2,1,0:T(8,128)S(1)}, f32[1,8,16,512]{3,2,1,0:T(8,128)}, u32[]{:S(2)}) copy-start(f32[1,8,16,512]{3,2,1,0:T(8,128)} %copy-done.1) | copy-start | bytes 786436
  667.7 11.4 %all-to-all-start.14 = ((f32[2,128,512]{2,0,1:T(2,128)}), f32[2,128,512]{2,0,1:T(2,128)S(1)}, u32[]{:S(2)}, u32[]{:S(2)}) async-start(f32[2,128,512]{2,0,1:T(2,128)} %copy.158), calls=%async_computation.14 | async-start | bytes 1048576 | tf_op jit(solution)/shard_map/all_to_all | solution.py:127
  700.1 17.3 %copy-start.18 = (f32[128,4]{1,0:T(8,128)S(1)}, f32[128,4]{1,0:T(8,128)}, u32[]{:S(2)}) copy-start(f32[128,4]{1,0:T(8,128)} %get-tuple-element.13) | copy-start | bytes 6148
  712.4 76.7 %all-to-all-start.15 = ((f32[8,1,16384]{2,1,0:T(1,128)}), f32[8,1,16384]{2,1,0:T(1,128)S(1)}, u32[]{:S(2)}, u32[]{:S(2)}) async-start(f32[8,1,16384]{2,1,0:T(1,128)} %reshape.610), calls=%async_computation.15 | async-start | bytes 1048576 | tf_op jit(solution)/shard_map/all_to_all | solution.py:128
  (20 other events, 231.1 us)
where the time goes:
time: 812 us; the launch traced here: 805 us
  local copies, waits for them, and re-layouts  281 us (35%)
  blocking collectives  189 us (23%)
  matrix products  183 us (23%)
  starting transfers between devices  82 us (10%)
  other arithmetic  36 us (4%)
  waiting for transfers between devices  31.1 us (4%)
    unnamed x64, local copies, waits for them, and re-layouts  120 us
    psum x1, blocking collectives, on_device(): total = lax.psum(sensitivity, ('az', 'dep'))  70 us
    ppermute x8, starting transfers between devices, padded_2(): lax.ppermute(head, axis, [((i + 1) % count, i) for i in range(count)])  62 us
    all_to_all x6, blocking collectives, on_device(): lax.all_to_all(propagate(deep), 'dep', split_axis=2, concat_axis=1, tiled...  59.7 us
    all_to_all x6, blocking collectives, on_device(): lax.all_to_all(couple(padded), 'dep', split_axis=1, concat_axis=2, tiled=...  59.7 us
    dot_general x32, matrix products, combine(): jnp.einsum(form, imag_part, cosine, precision=highest)  50 us
    dot_general x32, matrix products, combine(): jnp.einsum(form, imag_part, sine, precision=highest)  47.5 us
    dot_general x32, matrix products, combine(): jnp.einsum(form, real_part, cosine, precision=highest)  43 us
  transfers between devices with their start and end apart: 20, of which 16 were waited for; matrix products, arithmetic and copies ran while one was open for 7% of the time, Pallas kernels for 0%

commit v1 on v0

--- a/solution.py
+++ b/solution.py
@@ -1,3 +1,4 @@
+import functools
 import math
 import jax
 import jax.numpy as jnp
@@ -9,6 +10,15 @@
 radix_rows = 64
 label_block = 128
 highest = lax.Precision.HIGHEST
+
+
+def track_shelves(my_tile, bus_axis, mesh_ax):
+    for j in (bus_axis, mesh_ax):
+        my_tile = lax.psum(my_tile, j)
+    return my_tile
+
+
+get_shelves = functools.partial(track_shelves, bus_axis="dep", mesh_ax="az")
 
 
 def padded_2(cells, sides, width):
@@ -126,7 +136,7 @@
         padded = padded_2(rotate(field, cosine, sine), (("az", 1),), 2)
         deep = lax.all_to_all(couple(padded), "dep", split_axis=1, concat_axis=2, tiled=True)
         field = lax.all_to_all(propagate(deep), "dep", split_axis=2, concat_axis=1, tiled=True)
-    total = lax.psum(sensitivity, ("az", "dep"))
+    total = get_shelves(sensitivity)
     return (field, total)
 
 

time: 812 us -> 799 us (0.984)
  blocking collectives: 189 us -> 176 us
    psum x1 -> x2, blocking collectives: 70 us -> 56.9 us  [track_shelves(): my_tile = lax.psum(my_tile, j)]
where the time goes in v1:
time: 799 us; the launch traced here: 792 us
  local copies, waits for them, and re-layouts  281 us (35%)
  matrix products  183 us (23%)
  blocking collectives  176 us (22%)
  starting transfers between devices  81.9 us (10%)
  other arithmetic  37 us (5%)
  waiting for transfers between devices  30.8 us (4%)
    unnamed x64, local copies, waits for them, and re-layouts  120 us
    ppermute x8, starting transfers between devices, padded_2(): lax.ppermute(head, axis, [((i + 1) % count, i) for i in range(count)])  61.9 us
    all_to_all x6, blocking collectives, on_device(): lax.all_to_all(propagate(deep), 'dep', split_axis=2, concat_axis=1, tiled...  59.7 us
    all_to_all x6, blocking collectives, on_device(): lax.all_to_all(couple(padded), 'dep', split_axis=1, concat_axis=2, tiled=...  59.7 us
    psum x2, blocking collectives, track_shelves(): my_tile = lax.psum(my_tile, j)  56.9 us
    dot_general x32, matrix products, combine(): jnp.einsum(form, imag_part, cosine, precision=highest)  50 us
    dot_general x32, matrix products, combine(): jnp.einsum(form, imag_part, sine, precision=highest)  47.5 us
    dot_general x32, matrix products, combine(): jnp.einsum(form, real_part, cosine, precision=highest)  42.9 us
  transfers between devices with their start and end apart: 20, of which 16 were waited for; matrix products, arithmetic and copies ran while one was open for 7% of the time, Pallas kernels for 0%

profile of v1, /device:TPU:1, one launch (start us, length us, event | category | flops | bytes accessed | tf_op | source)
XLA Modules:
  0.0 792.4 jit_solution(4335563932589360800)
XLA Ops:
  58.6 10.0 %all_to_all.243 = f32[8,1,16384]{2,1,0:T(1,128)S(1)} all-to-all(f32[8,1,16384]{2,1,0:T(1,128)S(1)} %reshape.596), channel_id=1, replica_groups=mesh['az'=16,'dep'=8] {'dep'}, dimensions={0} | all-to-all | bytes 1048576 | tf_op jit(solution)/shard_map/all_to_all | solution.py:138
  83.9 8.8 %collective-permute-start.3 = (f32[2,2,512]{2,1,0:T(2,128)S(1)}, f32[2,2,512]{2,1,0:T(2,128)S(1)}, u32[]{:S(2)}, u32[]{:S(2)}) collective-permute-start(f32[2,2,512]{2,1,0:T(2,128)S(1)} %get-tuple-element.107), channel_id=1, source_target_pairs={{8,0},{16,8},{24,16},{32,24},{40,32},{48,40},{56,48},{64,56},{72,6... | collective-permute-start | bytes 24584 | tf_op jit(solution)/shard_map/ppermute | solution.py:33
  96.9 10.0 %all_to_all.244 = f32[2,128,512]{2,0,1:T(2,128)S(1)} all-to-all(f32[2,128,512]{2,0,1:T(2,128)S(1)} %copy.134), channel_id=1, replica_groups=mesh['az'=16,'dep'=8] {'dep'}, dimensions={1} | all-to-all | bytes 1048576 | tf_op jit(solution)/shard_map/all_to_all | solution.py:137
  141.2 10.0 %all_to_all.245 = f32[8,1,16384]{2,1,0:T(1,128)S(1)} all-to-all(f32[8,1,16384]{2,1,0:T(1,128)S(1)} %reshape.598), channel_id=1, replica_groups=mesh['az'=16,'dep'=8] {'dep'}, dimensions={0} | all-to-all | bytes 1048576 | tf_op jit(solution)/shard_map/all_to_all | solution.py:138
  166.0 8.7 %collective-permute-start.5 = (f32[2,2,512]{2,1,0:T(2,128)S(1)}, f32[2,2,512]{2,1,0:T(2,128)S(1)}, u32[]{:S(2)}, u32[]{:S(2)}) collective-permute-start(f32[2,2,512]{2,1,0:T(2,128)S(1)} %get-tuple-element.101), channel_id=1, source_target_pairs={{8,0},{16,8},{24,16},{32,24},{40,32},{48,40},{56,48},{64,56},{72,6... | collective-permute-start | bytes 24584 | tf_op jit(solution)/shard_map/ppermute | solution.py:33
  178.8 10.0 %all_to_all.246 = f32[2,128,512]{2,0,1:T(2,128)S(1)} all-to-all(f32[2,128,512]{2,0,1:T(2,128)S(1)} %copy.138), channel_id=1, replica_groups=mesh['az'=16,'dep'=8] {'dep'}, dimensions={1} | all-to-all | bytes 1048576 | tf_op jit(solution)/shard_map/all_to_all | solution.py:137
  228.4 10.0 %all_to_all.247 = f32[8,1,16384]{2,1,0:T(1,128)S(1)} all-to-all(f32[8,1,16384]{2,1,0:T(1,128)S(1)} %reshape.600), channel_id=1, replica_groups=mesh['az'=16,'dep'=8] {'dep'}, dimensions={0} | all-to-all | bytes 1048576 | tf_op jit(solution)/shard_map/all_to_all | solution.py:138
  253.2 8.7 %collective-permute-start.7 = (f32[2,2,512]{2,1,0:T(2,128)S(1)}, f32[2,2,512]{2,1,0:T(2,128)S(1)}, u32[]{:S(2)}, u32[]{:S(2)}) collective-permute-start(f32[2,2,512]{2,1,0:T(2,128)S(1)} %get-tuple-element.95), channel_id=1, source_target_pairs={{8,0},{16,8},{24,16},{32,24},{40,32},{48,40},{56,48},{64,56},{72,6... | collective-permute-start | bytes 24584 | tf_op jit(solution)/shard_map/ppermute | solution.py:33
  265.8 10.0 %all_to_all.248 = f32[2,128,512]{2,0,1:T(2,128)S(1)} all-to-all(f32[2,128,512]{2,0,1:T(2,128)S(1)} %copy.142), channel_id=1, replica_groups=mesh['az'=16,'dep'=8] {'dep'}, dimensions={1} | all-to-all | bytes 1048576 | tf_op jit(solution)/shard_map/all_to_all | solution.py:137
  319.1 10.0 %all_to_all.249 = f32[8,1,16384]{2,1,0:T(1,128)S(1)} all-to-all(f32[8,1,16384]{2,1,0:T(1,128)S(1)} %reshape.602), channel_id=1, replica_groups=mesh['az'=16,'dep'=8] {'dep'}, dimensions={0} | all-to-all | bytes 1048576 | tf_op jit(solution)/shard_map/all_to_all | solution.py:138
  343.9 8.5 %collective-permute-start.9 = (f32[2,2,512]{2,1,0:T(2,128)S(1)}, f32[2,2,512]{2,1,0:T(2,128)S(1)}, u32[]{:S(2)}, u32[]{:S(2)}) collective-permute-start(f32[2,2,512]{2,1,0:T(2,128)S(1)} %get-tuple-element.89), channel_id=1, source_target_pairs={{8,0},{16,8},{24,16},{32,24},{40,32},{48,40},{56,48},{64,56},{72,6... | collective-permute-start | bytes 24584 | tf_op jit(solution)/shard_map/ppermute | solution.py:33
  356.6 10.0 %all_to_all.250 = f32[2,128,512]{2,0,1:T(2,128)S(1)} all-to-all(f32[2,128,512]{2,0,1:T(2,128)S(1)} %copy.146), channel_id=1, replica_groups=mesh['az'=16,'dep'=8] {'dep'}, dimensions={1} | all-to-all | bytes 1048576 | tf_op jit(solution)/shard_map/all_to_all | solution.py:137
  409.9 10.0 %all_to_all.251 = f32[8,1,16384]{2,1,0:T(1,128)S(1)} all-to-all(f32[8,1,16384]{2,1,0:T(1,128)S(1)} %reshape.604), channel_id=1, replica_groups=mesh['az'=16,'dep'=8] {'dep'}, dimensions={0} | all-to-all | bytes 1048576 | tf_op jit(solution)/shard_map/all_to_all | solution.py:138
  434.7 8.7 %collective-permute-start.11 = (f32[2,2,512]{2,1,0:T(2,128)S(1)}, f32[2,2,512]{2,1,0:T(2,128)S(1)}, u32[]{:S(2)}, u32[]{:S(2)}) collective-permute-start(f32[2,2,512]{2,1,0:T(2,128)S(1)} %get-tuple-element.83), channel_id=1, source_target_pairs={{8,0},{16,8},{24,16},{32,24},{40,32},{48,40},{56,48},{64,56},{72,6... | collective-permute-start | bytes 24584 | tf_op jit(solution)/shard_map/ppermute | solution.py:33
  447.7 10.0 %all_to_all.252 = f32[2,128,512]{2,0,1:T(2,128)S(1)} all-to-all(f32[2,128,512]{2,0,1:T(2,128)S(1)} %copy.150), channel_id=1, replica_groups=mesh['az'=16,'dep'=8] {'dep'}, dimensions={1} | all-to-all | bytes 1048576 | tf_op jit(solution)/shard_map/all_to_all | solution.py:137
  501.0 10.0 %all_to_all.253 = f32[8,1,16384]{2,1,0:T(1,128)S(1)} all-to-all(f32[8,1,16384]{2,1,0:T(1,128)S(1)} %reshape.606), channel_id=1, replica_groups=mesh['az'=16,'dep'=8] {'dep'}, dimensions={0} | all-to-all | bytes 1048576 | tf_op jit(solution)/shard_map/all_to_all | solution.py:138
  525.8 8.7 %collective-permute-start.13 = (f32[2,2,512]{2,1,0:T(2,128)S(1)}, f32[2,2,512]{2,1,0:T(2,128)S(1)}, u32[]{:S(2)}, u32[]{:S(2)}) collective-permute-start(f32[2,2,512]{2,1,0:T(2,128)S(1)} %get-tuple-element.77), channel_id=1, source_target_pairs={{8,0},{16,8},{24,16},{32,24},{40,32},{48,40},{56,48},{64,56},{72,6... | collective-permute-start | bytes 24584 | tf_op jit(solution)/shard_map/ppermute | solution.py:33
  538.8 10.0 %all_to_all.254 = f32[2,128,512]{2,0,1:T(2,128)S(1)} all-to-all(f32[2,128,512]{2,0,1:T(2,128)S(1)} %copy.154), channel_id=1, replica_groups=mesh['az'=16,'dep'=8] {'dep'}, dimensions={1} | all-to-all | bytes 1048576 | tf_op jit(solution)/shard_map/all_to_all | solution.py:137
  585.0 7.9 reshape.608
  618.6 8.5 %collective-permute-start.15 = (f32[2,2,512]{2,1,0:T(2,128)S(1)}, f32[2,2,512]{2,1,0:T(2,128)S(1)}, u32[]{:S(2)}, u32[]{:S(2)}) collective-permute-start(f32[2,2,512]{2,1,0:T(2,128)S(1)} %get-tuple-element.71), channel_id=1, source_target_pairs={{8,0},{16,8},{24,16},{32,24},{40,32},{48,40},{56,48},{64,56},{72,6... | collective-permute-start | bytes 24584 | tf_op jit(solution)/shard_map/ppermute | solution.py:33
  704.9 7.9 reshape.610
  719.5 16.3 %psum.14 = f32[32]{0:T(128)S(1)} all-reduce(f32[32]{0:T(128)S(1)} %add_add_fusion), channel_id=1, replica_groups=mesh['az'=16,'dep'=8] {'dep'}, use_global_device_ids=true, to_apply=%region_8.9 | all-reduce | flops 32 | bytes 256 | tf_op jit(solution)/shard_map/psum | solution.py:17
  735.9 40.6 %psum.15 = f32[32]{0:T(128)} all-reduce(f32[32]{0:T(128)S(1)} %psum.14), channel_id=1, replica_groups=mesh['az'=16,'dep'=8] {'az'}, use_global_device_ids=true, to_apply=%region_9.10 | all-reduce | flops 32 | bytes 256 | tf_op jit(solution)/shard_map/psum | solution.py:17
  778.3 7.6 reshape.611
  (421 shorter events, 529.9 us)
Async XLA Ops:
  0.6 596.6 %copy-start = (f32[4096]{0:T(1024)S(1)}, f32[4096]{0:T(1024)}, u32[]{:S(2)}) copy-start(f32[4096]{0:T(1024)} %param.8) | copy-start | bytes 49156
  3.7 5.5 collective-permute-start.1
  5.2 6.7 collective-permute-start
  14.0 11.8 %all-to-all-start = ((f32[2,128,512]{2,0,1:T(2,128)}), f32[2,128,512]{2,0,1:T(2,128)S(1)}, u32[]{:S(2)}, u32[]{:S(2)}) async-start(f32[2,128,512]{2,0,1:T(2,128)} %pad_maximum_fusion.24), calls=%async_computation | async-start | bytes 1048576 | tf_op jit(solution)/shard_map/all_to_all | solution.py:137
  83.9 9.6 %collective-permute-start.3 = (f32[2,2,512]{2,1,0:T(2,128)S(1)}, f32[2,2,512]{2,1,0:T(2,128)S(1)}, u32[]{:S(2)}, u32[]{:S(2)}) collective-permute-start(f32[2,2,512]{2,1,0:T(2,128)S(1)} %get-tuple-element.107), channel_id=1, source_target_pairs={{8,0},{16,8},{24,16},{32,24},{40,32},{48,40},{56,48},{64,56},{72,6... | collective-permute-start | bytes 24584 | tf_op jit(solution)/shard_map/ppermute | solution.py:33
  92.7 3.3 collective-permute-start.2
  166.0 9.5 %collective-permute-start.5 = (f32[2,2,512]{2,1,0:T(2,128)S(1)}, f32[2,2,512]{2,1,0:T(2,128)S(1)}, u32[]{:S(2)}, u32[]{:S(2)}) collective-permute-start(f32[2,2,512]{2,1,0:T(2,128)S(1)} %get-tuple-element.101), channel_id=1, source_target_pairs={{8,0},{16,8},{24,16},{32,24},{40,32},{48,40},{56,48},{64,56},{72,6... | collective-permute-start | bytes 24584 | tf_op jit(solution)/shard_map/ppermute | solution.py:33
  174.6 3.2 collective-permute-start.4
  253.2 9.5 %collective-permute-start.7 = (f32[2,2,512]{2,1,0:T(2,128)S(1)}, f32[2,2,512]{2,1,0:T(2,128)S(1)}, u32[]{:S(2)}, u32[]{:S(2)}) collective-permute-start(f32[2,2,512]{2,1,0:T(2,128)S(1)} %get-tuple-element.95), channel_id=1, source_target_pairs={{8,0},{16,8},{24,16},{32,24},{40,32},{48,40},{56,48},{64,56},{72,6... | collective-permute-start | bytes 24584 | tf_op jit(solution)/shard_map/ppermute | solution.py:33
  261.8 3.0 collective-permute-start.6
  343.9 9.3 %collective-permute-start.9 = (f32[2,2,512]{2,1,0:T(2,128)S(1)}, f32[2,2,512]{2,1,0:T(2,128)S(1)}, u32[]{:S(2)}, u32[]{:S(2)}) collective-permute-start(f32[2,2,512]{2,1,0:T(2,128)S(1)} %get-tuple-element.89), channel_id=1, source_target_pairs={{8,0},{16,8},{24,16},{32,24},{40,32},{48,40},{56,48},{64,56},{72,6... | collective-permute-start | bytes 24584 | tf_op jit(solution)/shard_map/ppermute | solution.py:33
  352.4 3.3 collective-permute-start.8
  434.7 9.5 %collective-permute-start.11 = (f32[2,2,512]{2,1,0:T(2,128)S(1)}, f32[2,2,512]{2,1,0:T(2,128)S(1)}, u32[]{:S(2)}, u32[]{:S(2)}) collective-permute-start(f32[2,2,512]{2,1,0:T(2,128)S(1)} %get-tuple-element.83), channel_id=1, source_target_pairs={{8,0},{16,8},{24,16},{32,24},{40,32},{48,40},{56,48},{64,56},{72,6... | collective-permute-start | bytes 24584 | tf_op jit(solution)/shard_map/ppermute | solution.py:33
  443.3 3.4 collective-permute-start.10
  525.8 9.5 %collective-permute-start.13 = (f32[2,2,512]{2,1,0:T(2,128)S(1)}, f32[2,2,512]{2,1,0:T(2,128)S(1)}, u32[]{:S(2)}, u32[]{:S(2)}) collective-permute-start(f32[2,2,512]{2,1,0:T(2,128)S(1)} %get-tuple-element.77), channel_id=1, source_target_pairs={{8,0},{16,8},{24,16},{32,24},{40,32},{48,40},{56,48},{64,56},{72,6... | collective-permute-start | bytes 24584 | tf_op jit(solution)/shard_map/ppermute | solution.py:33
  534.4 3.5 collective-permute-start.12
  592.9 11.0 %all-to-all-start.13 = ((f32[8,1,16384]{2,1,0:T(1,128)}), f32[8,1,16384]{2,1,0:T(1,128)S(1)}, u32[]{:S(2)}, u32[]{:S(2)}) async-start(f32[8,1,16384]{2,1,0:T(1,128)} %reshape.608), calls=%async_computation.13 | async-start | bytes 1048576 | tf_op jit(solution)/shard_map/all_to_all | solution.py:138
  618.6 47.7 %collective-permute-start.15 = (f32[2,2,512]{2,1,0:T(2,128)S(1)}, f32[2,2,512]{2,1,0:T(2,128)S(1)}, u32[]{:S(2)}, u32[]{:S(2)}) collective-permute-start(f32[2,2,512]{2,1,0:T(2,128)S(1)} %get-tuple-element.71), channel_id=1, source_target_pairs={{8,0},{16,8},{24,16},{32,24},{40,32},{48,40},{56,48},{64,56},{72,6... | collective-permute-start | bytes 24584 | tf_op jit(solution)/shard_map/ppermute | solution.py:33
  627.1 39.2 %collective-permute-start.14 = (f32[2,2,512]{2,1,0:T(2,128)S(1)}, f32[2,2,512]{2,1,0:T(2,128)S(1)}, u32[]{:S(2)}, u32[]{:S(2)}) collective-permute-start(f32[2,2,512]{2,1,0:T(2,128)S(1)} %get-tuple-element.70), channel_id=1, source_target_pairs={{0,8},{8,16},{16,24},{24,32},{32,40},{40,48},{48,56},{56,64},{64,7... | collective-permute-start | bytes 24584 | tf_op jit(solution)/shard_map/ppermute | solution.py:31
  642.5 22.3 %copy-start.4 = (f32[1,8,16,512]{3,2,1,0:T(8,128)S(1)}, f32[1,8,16,512]{3,2,1,0:T(8,128)}, u32[]{:S(2)}) copy-start(f32[1,8,16,512]{3,2,1,0:T(8,128)} %copy-done.3) | copy-start | bytes 786436
  644.3 21.3 %copy-start.2 = (f32[1,8,16,512]{3,2,1,0:T(8,128)S(1)}, f32[1,8,16,512]{3,2,1,0:T(8,128)}, u32[]{:S(2)}) copy-start(f32[1,8,16,512]{3,2,1,0:T(8,128)} %copy-done.1) | copy-start | bytes 786436
  668.1 11.4 %all-to-all-start.14 = ((f32[2,128,512]{2,0,1:T(2,128)}), f32[2,128,512]{2,0,1:T(2,128)S(1)}, u32[]{:S(2)}, u32[]{:S(2)}) async-start(f32[2,128,512]{2,0,1:T(2,128)} %copy.158), calls=%async_computation.14 | async-start | bytes 1048576 | tf_op jit(solution)/shard_map/all_to_all | solution.py:137
  700.5 17.4 %copy-start.18 = (f32[128,4]{1,0:T(8,128)S(1)}, f32[128,4]{1,0:T(8,128)}, u32[]{:S(2)}) copy-start(f32[128,4]{1,0:T(8,128)} %get-tuple-element.13) | copy-start | bytes 6148
  712.8 63.6 %all-to-all-start.15 = ((f32[8,1,16384]{2,1,0:T(1,128)}), f32[8,1,16384]{2,1,0:T(1,128)S(1)}, u32[]{:S(2)}, u32[]{:S(2)}) async-start(f32[8,1,16384]{2,1,0:T(1,128)} %reshape.610), calls=%async_computation.15 | async-start | bytes 1048576 | tf_op jit(solution)/shard_map/all_to_all | solution.py:138
  (20 other events, 230.9 us)
